TPU v7x, 32 devices: a whole 2x2x4 slice. The times are simulated.
32 devices in a mesh: groups: 2 (over y), seq: 4 (over z), head: 4 (over x, core).
Axes of the slice: x: 2, y: 2, z: 4, core: 2. Of those that a mesh axis runs over, the one named last changes fastest.
Arguments:
- doc_start: int32 [1024], P(('groups', 'seq')), parts along dimension 0, may hold values from 0 to 511, as said below
- q_gdn: bfloat16 [1024, 2048], P(('groups', 'seq'), 'head'), parts along dimension 0, may hold values from -6 to 6
- k_gdn: bfloat16 [1024, 2048], P(('groups', 'seq'), 'head'), parts along dimension 0, may hold values from -6 to 6
- v_gdn: bfloat16 [1024, 4096], P(('groups', 'seq'), 'head'), parts along dimension 0, may hold values from -6 to 6
- z_gdn: bfloat16 [1024, 4096], P(('groups', 'seq'), 'head'), parts along dimension 0, may hold values from -6 to 6
- beta_logit: float32 [32, 1024], P('head', ('groups', 'seq')), parts along dimension 1, may hold values from -8 to 3
- log_decay: float32 [32, 1024], P('head', ('groups', 'seq')), parts along dimension 1, may hold values from -1 to 0
- norm_weight: float32 [128], replicated, may hold values from 0.1 to 1.9
- q_attn: bfloat16 [1024, 4096], P(('groups', 'seq'), 'head'), parts along dimension 0, may hold values from -6 to 6
- k_attn: bfloat16 [1024, 512], P(('groups', 'seq')), parts along dimension 0, may hold values from -6 to 6
- v_attn: bfloat16 [1024, 512], P(('groups', 'seq')), parts along dimension 0, may hold values from -6 to 6
- gate_attn: bfloat16 [1024, 4096], P(('groups', 'seq'), 'head'), parts along dimension 0, may hold values from -6 to 6
Outputs:
- gdn_out: bfloat16 [1024, 4096], P(('groups', 'seq'), 'head'), parts along dimension 0
- attn_out: bfloat16 [1024, 4096], P(('groups', 'seq'), 'head'), parts along dimension 0
There are 2 independent parts, one for each index of `groups`. A program takes and returns all parts, laid end to end along the dimension named above; an argument that names none is the same for every part. Nothing has to cross between parts.
Inputs may be any that keep to these rules, and one draw needn't show every extreme that they name: Nondecreasing; doc_start[i] <= i, with equality exactly at the first token of each of the 3 documents; the first document starts at 0.
All inputs are finite; a program needn't handle non-finite values.
Results may differ from a plain program's by a relative error of at most 0.0095.
Values may be sent and summed in bfloat16 or wider, within the bound.
A program may use at most 128 MiB of HBM per device.

v0:
```python
import jax
import jax.numpy as jnp
from jax import lax
from jax.sharding import PartitionSpec as P

DK = 128
DV = 128
QH = 16
KVH = 2
HD_A = 256
BLOCK = 64
HIGH = lax.Precision.HIGHEST


def shifted(shard, axis, by):
    length = lax.axis_size(axis)
    pairs = [(i, i + by) for i in range(length) if 0 <= i + by < length]
    return lax.ppermute(shard, axis, pairs)


def unit_rows(values):
    return values * lax.rsqrt(jnp.sum(values * values, axis=-1, keepdims=True) + 1e-06)


def blocked(values, count):
    length, heads, width = values.shape
    return values.reshape(count, length // count, heads, width).transpose(0, 2, 1, 3)


def block_terms(anchor, doc_block, query, keys, values, beta, log_gate):
    width = query.shape[1]
    running = jnp.cumsum(log_gate, axis=1)
    place = anchor + jnp.arange(width, dtype=jnp.int32)
    causal = place[None, :] <= place[:, None]
    same = causal & (doc_block[:, None] <= place[None, :])
    strict = same & (place[None, :] < place[:, None])
    spread = jnp.where(same[None], running[:, :, None] - running[:, None, :], 0.0)
    decay = jnp.where(same[None], jnp.exp(spread), 0.0)
    alive = (doc_block < anchor).astype(jnp.float32)
    entry = jnp.exp(running) * alive[None, :]
    gram = jnp.einsum("hik,hjk->hij", keys, keys, precision=HIGH)
    lower_part = jnp.where(strict[None], decay * gram, 0.0)
    system = jnp.eye(width, dtype=jnp.float32)[None] + beta[:, :, None] * lower_part
    right = jnp.concatenate([beta[:, :, None] * values, (beta * entry)[:, :, None] * keys], axis=2)
    solved = lax.linalg.triangular_solve(
        system, right, left_side=True, lower=True, unit_diagonal=True
    )
    fresh = solved[:, :, : values.shape[2]]
    erased = solved[:, :, values.shape[2] :]
    scores = jnp.einsum("hik,hjk->hij", query, keys, precision=HIGH) * decay
    local_out = jnp.einsum("hij,hjv->hiv", scores, fresh, precision=HIGH)
    reach = entry[:, :, None] * query - jnp.einsum("hij,hjk->hik", scores, erased, precision=HIGH)
    tail_keys = decay[:, -1, :, None] * keys
    identity = jnp.eye(keys.shape[2], dtype=jnp.float32)
    carry_map = entry[:, -1, None, None] * identity[None] - jnp.einsum(
        "hjk,hjl->hkl", erased, tail_keys, precision=HIGH
    )
    carry_add = jnp.einsum("hjv,hjk->hvk", fresh, tail_keys, precision=HIGH)
    return (local_out, reach, carry_map, carry_add)


def compose(earlier, later):
    joined_map = jnp.einsum("hkl,hlm->hkm", earlier[0], later[0], precision=HIGH)
    joined_add = jnp.einsum("hvl,hlm->hvm", earlier[1], later[0], precision=HIGH) + later[1]
    return (joined_map, joined_add)


def entering_state(device_map, device_add):

    def relay(turn, pair):
        incoming, state = pair
        incoming = shifted(state.astype(jnp.bfloat16), "seq", 1).astype(state.dtype)
        state = jnp.einsum("hvk,hkl->hvl", incoming, device_map, precision=HIGH) + device_add
        return (incoming, state)

    start_state, _ = lax.fori_loop(
        0, lax.axis_size("seq") - 1, relay, (jnp.zeros_like(device_add), device_add)
    )
    return start_state


def delta_layer(doc_start, q_gdn, k_gdn, v_gdn, z_gdn, beta_logit, log_decay, norm_weight, anchor):
    length = q_gdn.shape[0]
    key_heads = q_gdn.shape[1] // DK
    value_heads = v_gdn.shape[1] // DV
    repeat = value_heads // key_heads
    count = length // BLOCK
    query = jnp.repeat(
        unit_rows(q_gdn.astype(jnp.float32).reshape(length, key_heads, DK)), repeat, axis=1
    )
    keys = jnp.repeat(
        unit_rows(k_gdn.astype(jnp.float32).reshape(length, key_heads, DK)), repeat, axis=1
    )
    values = v_gdn.astype(jnp.float32).reshape(length, value_heads, DV)
    beta = jax.nn.sigmoid(beta_logit).reshape(value_heads, count, BLOCK).transpose(1, 0, 2)
    log_gate = log_decay.reshape(value_heads, count, BLOCK).transpose(1, 0, 2)
    docs = doc_start.reshape(count, BLOCK)
    anchors = anchor + BLOCK * jnp.arange(count, dtype=jnp.int32)
    identity = jnp.broadcast_to(jnp.eye(DK, dtype=jnp.float32), (value_heads, DK, DK))

    def sweep(totals, inputs):
        total_map, total_add = totals
        block_anchor, doc_block, q_block, k_block, v_block, b_block, g_block = inputs
        local_out, reach, carry_map, carry_add = block_terms(
            block_anchor, doc_block, q_block, k_block, v_block, b_block, g_block
        )
        joined = compose((total_map, total_add), (carry_map, carry_add))
        return (joined, (local_out, reach, total_map, total_add))

    start_totals = (identity, jnp.zeros((value_heads, DV, DK), jnp.float32))
    scanned = (
        anchors,
        docs,
        blocked(query, count),
        blocked(keys, count),
        blocked(values, count),
        beta,
        log_gate,
    )
    (device_map, device_add), (local_out, reach, prefix_map, prefix_add) = lax.scan(
        sweep, start_totals, scanned
    )
    start_state = entering_state(device_map, device_add)
    block_state = jnp.einsum("hvk,chkl->chvl", start_state, prefix_map, precision=HIGH) + prefix_add
    mixed = local_out + jnp.einsum("chik,chvk->chiv", reach, block_state, precision=HIGH)
    mixed = mixed.transpose(0, 2, 1, 3).reshape(length, value_heads, DV)
    gate = z_gdn.astype(jnp.float32).reshape(length, value_heads, DV)
    factor = lax.rsqrt(jnp.mean(mixed * mixed, axis=-1, keepdims=True) + 1e-06)
    normed = mixed * factor * norm_weight * jax.nn.silu(gate)
    return normed.reshape(length, value_heads * DV).astype(jnp.bfloat16)


def attend(doc_start, q_attn, k_attn, v_attn, gate_attn, anchor):
    length = q_attn.shape[0]
    local_heads = q_attn.shape[1] // HD_A
    group = QH // KVH
    shards_seen = lax.axis_size("seq") // 2 + 1
    window_size = shards_seen * length
    kv_head = lax.axis_index("head") * local_heads // group
    keys_own = lax.dynamic_slice_in_dim(k_attn, kv_head * HD_A, HD_A, 1)
    values_own = lax.dynamic_slice_in_dim(v_attn, kv_head * HD_A, HD_A, 1)
    query = q_attn.reshape(length, local_heads, HD_A)
    q_place = anchor + jnp.arange(length, dtype=jnp.int32)
    lower = jnp.maximum(doc_start, q_place - window_size + 1)
    lowest = jnp.min(lower)
    highest = anchor + length - 1
    factor = HD_A ** (-0.5)
    initial = (
        jnp.full((local_heads, length), -1e30, jnp.float32),
        jnp.zeros((local_heads, length), jnp.float32),
        jnp.zeros((local_heads, length, HD_A), jnp.float32),
    )
    key_piece = lax.all_gather(keys_own, "seq", axis=0, tiled=True)
    value_piece = lax.all_gather(values_own, "seq", axis=0, tiled=True)
    count = key_piece.shape[0]
    width = count
    while width > 1024 and width % 2 == 0:
        width = width // 2

    def one(index, inner):
        begin = index * width
        key_part = lax.dynamic_slice_in_dim(key_piece, begin, width, 0)
        value_part = lax.dynamic_slice_in_dim(value_piece, begin, width, 0)
        k_place = begin + jnp.arange(width, dtype=jnp.int32)

        def compute(state):
            peak, total, accum = state
            scores = (
                jnp.einsum("qhd,kd->hqk", query, key_part, preferred_element_type=jnp.float32)
                * factor
            )
            visible = (k_place[None, :] >= lower[:, None]) & (k_place[None, :] <= q_place[:, None])
            masked = jnp.where(visible[None], scores, -jnp.inf)
            new_peak = jnp.maximum(peak, jnp.max(masked, axis=-1))
            weights = jnp.exp(masked - new_peak[:, :, None])
            shrink = jnp.exp(peak - new_peak)
            total = total * shrink + jnp.sum(weights, axis=-1)
            update = jnp.einsum(
                "hqk,kd->hqd",
                weights.astype(jnp.bfloat16),
                value_part,
                preferred_element_type=jnp.float32,
            )
            accum = accum * shrink[:, :, None] + update
            return (new_peak, total, accum)

        def unchanged(state):
            return state

        busy = (begin <= highest) & (begin + width - 1 >= lowest)
        return lax.cond(busy, compute, unchanged, inner)

    peak, total, accum = lax.fori_loop(0, count // width, one, initial)
    mixed = (accum / total[:, :, None]).transpose(1, 0, 2).reshape(length, local_heads * HD_A)
    return (mixed * jax.nn.sigmoid(gate_attn.astype(jnp.float32))).astype(jnp.bfloat16)


def shards(
    doc_start,
    q_gdn,
    k_gdn,
    v_gdn,
    z_gdn,
    beta_logit,
    log_decay,
    norm_weight,
    q_attn,
    k_attn,
    v_attn,
    gate_attn,
):
    anchor = lax.axis_index("seq") * q_gdn.shape[0]
    gdn_out = delta_layer(
        doc_start, q_gdn, k_gdn, v_gdn, z_gdn, beta_logit, log_decay, norm_weight, anchor
    )
    attn_out = attend(doc_start, q_attn, k_attn, v_attn, gate_attn, anchor)
    return (gdn_out, attn_out)


def solution(mesh):
    return jax.shard_map(
        shards,
        mesh=mesh,
        in_specs=(
            P(("groups", "seq")),
            P(("groups", "seq"), "head"),
            P(("groups", "seq"), "head"),
            P(("groups", "seq"), "head"),
            P(("groups", "seq"), "head"),
            P("head", ("groups", "seq")),
            P("head", ("groups", "seq")),
            P(),
            P(("groups", "seq"), "head"),
            P(("groups", "seq"), None),
            P(("groups", "seq"), None),
            P(("groups", "seq"), "head"),
        ),
        out_specs=(P(("groups", "seq"), "head"), P(("groups", "seq"), "head")),
        check_vma=False,
    )
```

profile of v0, /device:TPU:0, one launch (start us, length us, event | category | flops | bytes accessed | tf_op | source)
XLA Modules:
  0.0 189.3 jit_solution(7092509554987152704)
XLA Ops:
  0.7 1.0 reshape.347
  2.2 0.9 copy-done.16
  3.7 0.9 copy-done.13
  4.7 0.8 bitcast_bitcast_fusion
  5.7 0.6 copy-done.19
  6.4 0.6 copy-done.18
  7.1 0.7 copy-done.21
  7.8 105.6 %while.13 = (s32[]{:T(128)}, f32[8,128,128]{1,2,0:T(8,128)S(1)}, f32[8,128,128]{1,2,0:T(8,128)S(1)}, f32[2,8,64,128]{3,2,1,0:T(8,128)}, f32[2,8,64,128]{3,2,1,0:...) while((s32[]{:T(128)}, f32[8,128,128]{1,2,0:T(8,128)S(1)}, ...), condition=%wide.region_4.5_spmd.clone, body=%wide.region_2.4_spmd.clone.sunk | while | flops 907780864 | bytes 40192524 | solution.py:120
  7.8 0.6 dynamic_slice.99
  8.4 0.6 iota_add_fusion.5
  9.5 0.6 fusion.124
  10.1 39.3 %custom-call.11 = f32[8,1,64,64]{2,3,1,0:T(8,128)S(1)} custom-call(f32[8,1,64,64]{3,2,1,0:T(8,128)S(1)} %fusion.124), custom_call_target="InvertDiagBlocksLowerTriangular" | custom-call | tf_op jit(solution)/shard_map/while/body/eval_jaxpr/triangular_solve | solution.py:45
  49.4 0.7 fusion.120
  50.3 1.0 constant_dynamic-slice_fusion.9
  51.4 0.6 fusion.125
  52.4 1.1 convolution_subtract_fusion.3
  53.5 1.0 convolution_bitcast_fusion.7
  55.2 1.1 convolution_add_fusion.7
  56.3 1.0 convolution_bitcast_fusion.6
  57.4 0.6 convolution_multiply_fusion.4
  57.9 0.5 copy-done.10
  58.4 0.4 fusion.127
  58.8 0.6 copy-done.7
  59.8 0.8 copy-done.8
  60.6 0.6 dynamic_slice.99
  61.2 0.6 iota_add_fusion.5
  62.3 0.6 fusion.124
  62.9 39.3 %custom-call.11 = f32[8,1,64,64]{2,3,1,0:T(8,128)S(1)} custom-call(f32[8,1,64,64]{3,2,1,0:T(8,128)S(1)} %fusion.124), custom_call_target="InvertDiagBlocksLowerTriangular" | custom-call | tf_op jit(solution)/shard_map/while/body/eval_jaxpr/triangular_solve | solution.py:45
  102.2 0.7 fusion.120
  103.1 1.0 constant_dynamic-slice_fusion.9
  104.2 0.6 fusion.125
  105.2 1.1 convolution_subtract_fusion.3
  106.3 1.0 convolution_bitcast_fusion.7
  108.0 1.1 convolution_add_fusion.7
  109.1 1.0 convolution_bitcast_fusion.6
  110.2 0.6 convolution_multiply_fusion.4
  110.7 0.5 copy-done.10
  111.6 0.6 copy-done.7
  112.7 0.8 copy-done.8
  113.6 0.7 convert.19
  114.6 34.6 %while.12 = (s32[]{:T(128)}, f32[8,128,128]{2,1,0:T(8,128)}, bf16[8,128,128]{2,1,0:T(8,128)(2,1)}, f32[8,128,128]{2,1,0:T(8,128)S(1)}, f32[8,128,128]{2,1,0:T(8,128)S(1)}, /*index=5*/s32[]{:T(128)}) while((s32[]{:T(128)}, f32[8,128,128]{2,1,0:T(8,128)}, bf16[8,128,128]{2,1,0:T(8,128)(2,1)}, f32[8,128,128]{2,1,0:T(8,128)S(1)}, ...), condition=%wide.region_6.7_spmd, body=%wide.region_5.6_spmd.sunk | while | flops 201719808 | bytes 3407981 | solution.py:76
  114.6 5.1 %collective-permute-start = (bf16[8,128,128]{2,1,0:T(8,128)(2,1)}, bf16[8,128,128]{2,1,0:T(8,128)(2,1)S(1)}, u32[]{:S(2)}, u32[]{:S(2)}) collective-permute-start(bf16[8,128,128]{2,1,0:T(8,128)(2,1)} %get-tuple-element.581), channel_id=1, source_target_pairs={{0,4},{4,8},{8,12},{1,5},{5,9},{9,13},{2,6},{6,10},{10,14},{3,7},{... | collective-permute-start | bytes 786440 | tf_op jit(solution)/shard_map/while/body/eval_jaxpr/ppermute | solution.py:18
  119.8 5.8 %collective-permute-done = bf16[8,128,128]{2,1,0:T(8,128)(2,1)S(1)} collective-permute-done((bf16[8,128,128]{2,1,0:T(8,128)(2,1)}, bf16[8,128,128]{2,1,0:T(8,128)(2,1)S(1)}, u32[]{:S(2)}, u32[]{:S(2)}) %collective-permute-start) | collective-permute-done | bytes 262176 | tf_op jit(solution)/shard_map/while/body/eval_jaxpr/ppermute | solution.py:18
  125.6 0.8 convert_element_type.81
  126.4 1.1 convolution_add_fusion.6
  127.5 4.3 %collective-permute-start = (bf16[8,128,128]{2,1,0:T(8,128)(2,1)}, bf16[8,128,128]{2,1,0:T(8,128)(2,1)S(1)}, u32[]{:S(2)}, u32[]{:S(2)}) collective-permute-start(bf16[8,128,128]{2,1,0:T(8,128)(2,1)} %get-tuple-element.581), channel_id=1, source_target_pairs={{0,4},{4,8},{8,12},{1,5},{5,9},{9,13},{2,6},{6,10},{10,14},{3,7},{... | collective-permute-start | bytes 786440 | tf_op jit(solution)/shard_map/while/body/eval_jaxpr/ppermute | solution.py:18
  131.8 5.0 %collective-permute-done = bf16[8,128,128]{2,1,0:T(8,128)(2,1)S(1)} collective-permute-done((bf16[8,128,128]{2,1,0:T(8,128)(2,1)}, bf16[8,128,128]{2,1,0:T(8,128)(2,1)S(1)}, u32[]{:S(2)}, u32[]{:S(2)}) %collective-permute-start) | collective-permute-done | bytes 262176 | tf_op jit(solution)/shard_map/while/body/eval_jaxpr/ppermute | solution.py:18
  136.8 0.8 convert_element_type.81
  137.7 1.1 convolution_add_fusion.6
  138.8 4.3 %collective-permute-start = (bf16[8,128,128]{2,1,0:T(8,128)(2,1)}, bf16[8,128,128]{2,1,0:T(8,128)(2,1)S(1)}, u32[]{:S(2)}, u32[]{:S(2)}) collective-permute-start(bf16[8,128,128]{2,1,0:T(8,128)(2,1)} %get-tuple-element.581), channel_id=1, source_target_pairs={{0,4},{4,8},{8,12},{1,5},{5,9},{9,13},{2,6},{6,10},{10,14},{3,7},{... | collective-permute-start | bytes 786440 | tf_op jit(solution)/shard_map/while/body/eval_jaxpr/ppermute | solution.py:18
  143.1 4.2 %collective-permute-done = bf16[8,128,128]{2,1,0:T(8,128)(2,1)S(1)} collective-permute-done((bf16[8,128,128]{2,1,0:T(8,128)(2,1)}, bf16[8,128,128]{2,1,0:T(8,128)(2,1)S(1)}, u32[]{:S(2)}, u32[]{:S(2)}) %collective-permute-start) | collective-permute-done | bytes 262176 | tf_op jit(solution)/shard_map/while/body/eval_jaxpr/ppermute | solution.py:18
  147.2 0.8 convert_element_type.81
  148.1 1.1 convolution_add_fusion.6
  149.2 2.2 %fusion.53 = f32[2,8,128,128]{2,3,1,0:T(8,128)S(1)} fusion(f32[2,8,128,128]{2,3,1,0:T(8,128)S(1)} %copy-done.6, f32[2,8,128,128]{2,3,1,0:T(8,128)S(1)} %copy-done.3, f32[8,128,128]{2,1,0:T(8,128)} %get-tuple-element.215), kind=kOutput, calls=%fused_computation.91 | convolution fusion | flops 402915328 | bytes 3670016 | tf_op jit(solution)/shard_map/hvk,chkl->chvl/dot_general | solution.py:124
  151.4 1.1 multiply_reduce_fusion
  153.2 0.6 copy-done.20
  153.9 1.0 fusion.61
  154.9 15.6 %all_gather.6 = bf16[512,256]{1,0:T(8,128)(2,1)S(1)} all-gather(bf16[128,256]{1,0:T(8,128)(2,1)S(1)} %constant_dynamic-slice_fusion.5), channel_id=1, replica_groups=mesh['groups'=2,'seq'=4,'head'=4] {'seq'}, dimensions={0}, use_global_device_ids=true | all-gather | bytes 327680 | tf_op jit(solution)/shard_map/all_gather | solution.py:153
  170.5 14.0 %all_gather.7 = bf16[512,256]{1,0:T(8,128)(2,1)S(1)} all-gather(bf16[128,256]{1,0:T(8,128)(2,1)S(1)} %constant_dynamic-slice_fusion.4), channel_id=1, replica_groups=mesh['groups'=2,'seq'=4,'head'=4] {'seq'}, dimensions={0}, use_global_device_ids=true | all-gather | bytes 327680 | tf_op jit(solution)/shard_map/all_gather | solution.py:154
  184.5 0.6 fusion.64
  186.1 1.2 conditional.1
  186.9 0.5 convolution_add_fusion.1
  187.6 0.9 copy-done.15
  188.5 0.8 multiply_convert_fusion
  (127 shorter events, 8.1 us)
Async XLA Ops:
  0.6 154.2 %copy-start = (bf16[128,512]{1,0:T(8,128)(2,1)S(1)}, bf16[128,512]{1,0:T(8,128)(2,1)}, u32[]{:S(2)}) copy-start(bf16[128,512]{1,0:T(8,128)(2,1)} %param.27) | copy-start | bytes 393220
  2.2 0.9 copy-start.16
  3.6 1.0 copy-start.13
  5.6 0.7 copy-start.19
  6.3 0.7 copy-start.18
  7.1 0.7 copy-start.21
  53.5 1.2 copy-start.1
  53.5 1.5 copy-start.4
  55.1 2.2 %copy-start.2 = (f32[2,8,128,128]{2,3,1,0:T(8,128)}, f32[2,8,128,128]{2,3,1,0:T(8,128)S(1)}, u32[]{:S(2)}) copy-start(f32[2,8,128,128]{2,3,1,0:T(8,128)S(1)} %get-tuple-element.561) | copy-start | bytes 3145732 | tf_op jit(solution)/shard_map/while
  55.2 2.2 %copy-start.5 = (f32[2,8,128,128]{2,3,1,0:T(8,128)}, f32[2,8,128,128]{2,3,1,0:T(8,128)S(1)}, u32[]{:S(2)}) copy-start(f32[2,8,128,128]{2,3,1,0:T(8,128)S(1)} %get-tuple-element.562) | copy-start | bytes 3145732 | tf_op jit(solution)/shard_map/while
  57.3 1.0 copy-start.10
  58.4 1.0 copy-start.7
  58.8 1.0 copy-start.11
  59.8 0.8 copy-start.8
  106.3 1.2 copy-start.1
  106.3 1.5 copy-start.4
  108.0 2.2 %copy-start.2 = (f32[2,8,128,128]{2,3,1,0:T(8,128)}, f32[2,8,128,128]{2,3,1,0:T(8,128)S(1)}, u32[]{:S(2)}) copy-start(f32[2,8,128,128]{2,3,1,0:T(8,128)S(1)} %get-tuple-element.561) | copy-start | bytes 3145732 | tf_op jit(solution)/shard_map/while
  108.0 2.2 %copy-start.5 = (f32[2,8,128,128]{2,3,1,0:T(8,128)}, f32[2,8,128,128]{2,3,1,0:T(8,128)S(1)}, u32[]{:S(2)}) copy-start(f32[2,8,128,128]{2,3,1,0:T(8,128)S(1)} %get-tuple-element.562) | copy-start | bytes 3145732 | tf_op jit(solution)/shard_map/while
  110.2 1.0 copy-start.10
  111.2 1.0 copy-start.7
  111.6 1.0 copy-start.11
  112.6 0.8 copy-start.8
  114.6 34.6 %copy-start.3 = (f32[2,8,128,128]{2,3,1,0:T(8,128)S(1)}, f32[2,8,128,128]{2,3,1,0:T(8,128)}, u32[]{:S(2)}) copy-start(f32[2,8,128,128]{2,3,1,0:T(8,128)} %get-tuple-element.212) | copy-start | bytes 3145732
  114.6 34.6 %copy-start.6 = (f32[2,8,128,128]{2,3,1,0:T(8,128)S(1)}, f32[2,8,128,128]{2,3,1,0:T(8,128)}, u32[]{:S(2)}) copy-start(f32[2,8,128,128]{2,3,1,0:T(8,128)} %get-tuple-element.216) | copy-start | bytes 3145732
  114.6 11.0 %collective-permute-start = (bf16[8,128,128]{2,1,0:T(8,128)(2,1)}, bf16[8,128,128]{2,1,0:T(8,128)(2,1)S(1)}, u32[]{:S(2)}, u32[]{:S(2)}) collective-permute-start(bf16[8,128,128]{2,1,0:T(8,128)(2,1)} %get-tuple-element.581), channel_id=1, source_target_pairs={{0,4},{4,8},{8,12},{1,5},{5,9},{9,13},{2,6},{6,10},{10,14},{3,7},{... | collective-permute-start | bytes 786440 | tf_op jit(solution)/shard_map/while/body/eval_jaxpr/ppermute | solution.py:18
  127.5 9.3 %collective-permute-start = (bf16[8,128,128]{2,1,0:T(8,128)(2,1)}, bf16[8,128,128]{2,1,0:T(8,128)(2,1)S(1)}, u32[]{:S(2)}, u32[]{:S(2)}) collective-permute-start(bf16[8,128,128]{2,1,0:T(8,128)(2,1)} %get-tuple-element.581), channel_id=1, source_target_pairs={{0,4},{4,8},{8,12},{1,5},{5,9},{9,13},{2,6},{6,10},{10,14},{3,7},{... | collective-permute-start | bytes 786440 | tf_op jit(solution)/shard_map/while/body/eval_jaxpr/ppermute | solution.py:18
  138.8 8.5 %collective-permute-start = (bf16[8,128,128]{2,1,0:T(8,128)(2,1)}, bf16[8,128,128]{2,1,0:T(8,128)(2,1)S(1)}, u32[]{:S(2)}, u32[]{:S(2)}) collective-permute-start(bf16[8,128,128]{2,1,0:T(8,128)(2,1)} %get-tuple-element.581), channel_id=1, source_target_pairs={{0,4},{4,8},{8,12},{1,5},{5,9},{9,13},{2,6},{6,10},{10,14},{3,7},{... | collective-permute-start | bytes 786440 | tf_op jit(solution)/shard_map/while/body/eval_jaxpr/ppermute | solution.py:18
  149.2 2.2 %copy-start.9 = (f32[2,8,64,128]{3,2,1,0:T(8,128)S(1)}, f32[2,8,64,128]{3,2,1,0:T(8,128)}, u32[]{:S(2)}) copy-start(f32[2,8,64,128]{3,2,1,0:T(8,128)} %get-tuple-element.210) | copy-start | bytes 1572868
  149.2 2.2 %copy-start.12 = (f32[2,8,64,128]{3,2,1,0:T(8,128)S(1)}, f32[2,8,64,128]{3,2,1,0:T(8,128)}, u32[]{:S(2)}) copy-start(f32[2,8,64,128]{3,2,1,0:T(8,128)} %get-tuple-element.211) | copy-start | bytes 1572868
  152.9 1.0 copy-start.14
  153.2 0.7 copy-start.20
  154.9 15.6 %copy-start.17 = (bf16[128,512]{1,0:T(8,128)(2,1)S(1)}, bf16[128,512]{1,0:T(8,128)(2,1)}, u32[]{:S(2)}) copy-start(bf16[128,512]{1,0:T(8,128)(2,1)} %param.28) | copy-start | bytes 393220
  185.2 0.9 copy-start.22
  187.5 1.0 copy-start.15
where the time goes:
time: 190 us; the launch traced here: 189 us
  other arithmetic  90.3 us (48%)
  blocking collectives  29.7 us (16%)
  matrix products  21.1 us (11%)
  local copies, waits for them, and re-layouts  17.3 us (9%)
  waiting for transfers between devices  15 us (8%)
  starting transfers between devices  13.7 us (7%)
    another operation x6, other arithmetic, block_terms(): lax.linalg.triangular_solve(system, right, left_side=True, lower=True, un...  78.8 us
    all_gather x1, blocking collectives, attend(): key_piece = lax.all_gather(keys_own, 'seq', axis=0, tiled=True)  15.6 us
    ppermute x3, waiting for transfers between devices, shifted(): return lax.ppermute(shard, axis, pairs)  15 us
    all_gather x1, blocking collectives, attend(): value_piece = lax.all_gather(values_own, 'seq', axis=0, tiled=True)  14 us
    ppermute x3, starting transfers between devices, shifted(): return lax.ppermute(shard, axis, pairs)  13.7 us
    unnamed x31, local copies, waits for them, and re-layouts  5.57 us
    while x34, local copies, waits for them, and re-layouts  4.8 us
  transfers between devices with their start and end apart: 3, of which 3 were waited for; matrix products, arithmetic and copies ran while one was open for 0% of the time, Pallas kernels for 0%

commit v1 on v0

--- a/solution.py
+++ b/solution.py
@@ -10,6 +10,18 @@
 HD_A = 256
 BLOCK = 64
 HIGH = lax.Precision.HIGHEST
+
+
+def collect(array, axis, dim):
+    ways, here = (lax.axis_size(axis), lax.axis_index(axis))
+    grown, reach = (array, 1)
+    while reach < ways:
+        theirs = lax.ppermute(grown, axis, [(d, d ^ reach) for d in range(ways)])
+        mine_first = jnp.concatenate([grown, theirs], axis=dim)
+        theirs_first = jnp.concatenate([theirs, grown], axis=dim)
+        grown = jnp.where(here & reach == 0, mine_first, theirs_first)
+        reach = 2 * reach
+    return grown
 
 
 def shifted(shard, axis, by):
@@ -151,7 +163,7 @@
         jnp.zeros((local_heads, length, HD_A), jnp.float32),
     )
     key_piece = lax.all_gather(keys_own, "seq", axis=0, tiled=True)
-    value_piece = lax.all_gather(values_own, "seq", axis=0, tiled=True)
+    value_piece = collect(values_own, "seq", 0)
     count = key_piece.shape[0]
     width = count
     while width > 1024 and width % 2 == 0:

time: 190 us -> 182 us (0.958)
  blocking collectives: 29.7 us -> 13.8 us
  starting transfers between devices: 13.7 us -> 18.8 us
  matrix products: 21.1 us -> 24.7 us
    all_gather x1 -> x0, blocking collectives: 14 us -> none  [attend(): value_piece = lax.all_gather(values_own, 'seq', axis=0, tiled=True)]
    ppermute x0 -> x2, starting transfers between devices: none -> 7.51 us  [collect(): theirs = lax.ppermute(grown, axis, [(d, d ^ reach) for d in range(ways)])]
    ppermute x3, starting transfers between devices: 13.7 us -> 11.2 us  [shifted(): return lax.ppermute(shard, axis, pairs)]
    dot_general x3, matrix products: 3.32 us -> 1.2 us  [relay(): jnp.einsum('hvk,hkl->hvl', incoming, device_map, precision=HIGH)]
    unnamed x31 -> x29, local copies, waits for them, and re-layouts: 5.57 us -> 7 us
    while x34 -> x50, local copies, waits for them, and re-layouts: 4.8 us -> 3.54 us
  transfers between devices with their start and end apart: 3 -> 5, of which waited for: 3 -> 3; matrix products, arithmetic and copies ran while one was open for 0% -> 65% of each run, Pallas kernels for 0% -> 0%
where the time goes in v1:
time: 182 us; the launch traced here: 181 us
  other arithmetic  91.5 us (50%)
  matrix products  24.7 us (14%)
  starting transfers between devices  18.8 us (10%)
  local copies, waits for them, and re-layouts  16.5 us (9%)
  waiting for transfers between devices  13.8 us (8%)
  blocking collectives  13.8 us (8%)
    another operation x6, other arithmetic, block_terms(): lax.linalg.triangular_solve(system, right, left_side=True, lower=True, un...  80.3 us
    all_gather x1, blocking collectives, attend(): key_piece = lax.all_gather(keys_own, 'seq', axis=0, tiled=True)  13.8 us
    ppermute x3, waiting for transfers between devices, shifted(): return lax.ppermute(shard, axis, pairs)  13.8 us
    ppermute x3, starting transfers between devices, shifted(): return lax.ppermute(shard, axis, pairs)  11.2 us
    ppermute x2, starting transfers between devices, collect(): theirs = lax.ppermute(grown, axis, [(d, d ^ reach) for d in range(ways)])  7.51 us
    unnamed x29, local copies, waits for them, and re-layouts  7 us
  transfers between devices with their start and end apart: 5, of which 3 were waited for; matrix products, arithmetic and copies ran while one was open for 65% of the time, Pallas kernels for 0%

profile of v1, /device:TPU:0, one launch (start us, length us, event | category | flops | bytes accessed | tf_op | source)
XLA Modules:
  0.0 181.5 jit_solution(8703834445420237085)
XLA Ops:
  0.7 0.9 copy-done
  1.5 0.6 constant_dynamic-slice_fusion.4
  2.2 3.1 %collective-permute-start.1 = (bf16[128,256]{1,0:T(8,128)(2,1)}, bf16[128,256]{1,0:T(8,128)(2,1)}, u32[]{:S(2)}, u32[]{:S(2)}) collective-permute-start(bf16[128,256]{1,0:T(8,128)(2,1)} %constant_dynamic-slice_fusion.4), channel_id=1, source_target_pairs={{0,4},{4,0},{8,12},{12,8},{1,5},{5,1},{9,13},{13,9},{2,6},{6,2},{1... | collective-permute-start | bytes 196616 | tf_op jit(solution)/shard_map/ppermute | solution.py:19
  5.3 0.6 copy-done.22
  5.9 1.2 fusion.66
  7.8 0.9 copy-done.12
  9.2 0.9 copy-done.8
  10.4 0.6 copy-done.19
  11.1 0.6 copy-done.18
  11.7 0.7 reshape.336
  12.5 109.1 %while.13 = (s32[]{:T(128)}, f32[8,128,128]{1,2,0:T(8,128)S(1)}, f32[8,128,128]{1,2,0:T(8,128)S(1)}, f32[2,8,64,128]{3,2,1,0:T(8,128)}, f32[2,8,64,128]{3,2,1,0:...) while((s32[]{:T(128)}, f32[8,128,128]{1,2,0:T(8,128)S(1)}, ...), condition=%wide.region_4.5_spmd.clone, body=%wide.region_2.4_spmd.clone.sunk | while | flops 907780864 | bytes 36036276 | solution.py:132
  12.5 0.5 copy-done.24
  13.1 0.6 dynamic_slice.99
  13.7 0.6 iota_add_fusion.5
  14.4 0.7 constant_dynamic-slice_fusion.8
  15.4 1.3 fusion.126
  16.7 40.0 %custom-call.11 = f32[8,1,64,64]{2,3,1,0:T(8,128)S(1)} custom-call(f32[8,1,64,64]{3,2,1,0:T(8,128)} %fusion.126), custom_call_target="InvertDiagBlocksLowerTriangular" | custom-call | tf_op jit(solution)/shard_map/while/body/eval_jaxpr/triangular_solve | solution.py:57
  56.7 0.6 fusion.122
  57.7 0.7 fusion.127
  58.7 1.1 convolution_subtract_fusion.3
  59.8 1.0 convolution_bitcast_fusion.7
  61.5 1.1 convolution_add_fusion.7
  62.6 1.0 convolution_bitcast_fusion.6
  63.6 0.6 convolution_multiply_fusion.4
  64.2 1.1 fusion.129
  65.3 1.1 fusion.128
  66.4 0.7 copy-done.14
  67.1 0.5 copy-done.24
  67.7 0.6 dynamic_slice.99
  68.2 0.6 iota_add_fusion.5
  68.9 0.7 constant_dynamic-slice_fusion.8
  69.9 1.3 fusion.126
  71.2 40.0 %custom-call.11 = f32[8,1,64,64]{2,3,1,0:T(8,128)S(1)} custom-call(f32[8,1,64,64]{3,2,1,0:T(8,128)} %fusion.126), custom_call_target="InvertDiagBlocksLowerTriangular" | custom-call | tf_op jit(solution)/shard_map/while/body/eval_jaxpr/triangular_solve | solution.py:57
  111.3 0.6 fusion.122
  112.2 0.7 fusion.127
  113.3 1.1 convolution_subtract_fusion.3
  114.4 1.0 convolution_bitcast_fusion.7
  116.0 1.1 convolution_add_fusion.7
  117.1 1.0 convolution_bitcast_fusion.6
  118.2 0.6 convolution_multiply_fusion.4
  118.7 1.1 fusion.129
  119.8 1.1 fusion.128
  120.9 0.7 copy-done.14
  122.1 28.8 %while.12 = (s32[]{:T(128)}, f32[8,128,128]{2,1,0:T(8,128)}, bf16[8,128,128]{2,1,0:T(8,128)(2,1)S(1)}, f32[8,128,128]{2,1,0:T(8,128)S(1)}, f32[8,128,128]{2,1,0:T(8,128)S(1)}, /*index=5*/s32[]{:T(128)}) while((s32[]{:T(128)}, f32[8,128,128]{2,1,0:T(8,128)}, bf16[8,128,128]{2,1,0:T(8,128)(2,1)S(1)}, f32[8,128,128]{2,1,0:T(8,128)S(1)}, ...), condition=%wide.region_6.7_spmd, body=%wide.region_5.6_spmd.sunk | while | flops 201719808 | bytes 3407981 | solution.py:88
  122.1 2.1 %collective-permute-start = (bf16[8,128,128]{2,1,0:T(8,128)(2,1)S(1)}, bf16[8,128,128]{2,1,0:T(8,128)(2,1)S(1)}, u32[]{:S(2)}, u32[]{:S(2)}) collective-permute-start(bf16[8,128,128]{2,1,0:T(8,128)(2,1)S(1)} %get-tuple-element.606), channel_id=1, source_target_pairs={{0,4},{4,8},{8,12},{1,5},{5,9},{9,13},{2,6},{6,10},{10,14},{3,7},{... | collective-permute-start | bytes 786440 | tf_op jit(solution)/shard_map/while/body/eval_jaxpr/ppermute | solution.py:30
  124.2 5.5 %collective-permute-done = bf16[8,128,128]{2,1,0:T(8,128)(2,1)S(1)} collective-permute-done((bf16[8,128,128]{2,1,0:T(8,128)(2,1)S(1)}, bf16[8,128,128]{2,1,0:T(8,128)(2,1)S(1)}, u32[]{:S(2)}, u32[]{:S(2)}) %collective-permute-start) | collective-permute-done | bytes 262176 | tf_op jit(solution)/shard_map/while/body/eval_jaxpr/ppermute | solution.py:30
  129.7 0.8 convert_element_type.81
  130.9 4.8 %collective-permute-start = (bf16[8,128,128]{2,1,0:T(8,128)(2,1)S(1)}, bf16[8,128,128]{2,1,0:T(8,128)(2,1)S(1)}, u32[]{:S(2)}, u32[]{:S(2)}) collective-permute-start(bf16[8,128,128]{2,1,0:T(8,128)(2,1)S(1)} %get-tuple-element.606), channel_id=1, source_target_pairs={{0,4},{4,8},{8,12},{1,5},{5,9},{9,13},{2,6},{6,10},{10,14},{3,7},{... | collective-permute-start | bytes 786440 | tf_op jit(solution)/shard_map/while/body/eval_jaxpr/ppermute | solution.py:30
  135.8 4.4 %collective-permute-done = bf16[8,128,128]{2,1,0:T(8,128)(2,1)S(1)} collective-permute-done((bf16[8,128,128]{2,1,0:T(8,128)(2,1)S(1)}, bf16[8,128,128]{2,1,0:T(8,128)(2,1)S(1)}, u32[]{:S(2)}, u32[]{:S(2)}) %collective-permute-start) | collective-permute-done | bytes 262176 | tf_op jit(solution)/shard_map/while/body/eval_jaxpr/ppermute | solution.py:30
  140.1 0.8 convert_element_type.81
  141.4 4.4 %collective-permute-start = (bf16[8,128,128]{2,1,0:T(8,128)(2,1)S(1)}, bf16[8,128,128]{2,1,0:T(8,128)(2,1)S(1)}, u32[]{:S(2)}, u32[]{:S(2)}) collective-permute-start(bf16[8,128,128]{2,1,0:T(8,128)(2,1)S(1)} %get-tuple-element.606), channel_id=1, source_target_pairs={{0,4},{4,8},{8,12},{1,5},{5,9},{9,13},{2,6},{6,10},{10,14},{3,7},{... | collective-permute-start | bytes 786440 | tf_op jit(solution)/shard_map/while/body/eval_jaxpr/ppermute | solution.py:30
  145.8 3.9 %collective-permute-done = bf16[8,128,128]{2,1,0:T(8,128)(2,1)S(1)} collective-permute-done((bf16[8,128,128]{2,1,0:T(8,128)(2,1)S(1)}, bf16[8,128,128]{2,1,0:T(8,128)(2,1)S(1)}, u32[]{:S(2)}, u32[]{:S(2)}) %collective-permute-start) | collective-permute-done | bytes 262176 | tf_op jit(solution)/shard_map/while/body/eval_jaxpr/ppermute | solution.py:30
  149.7 0.8 convert_element_type.81
  150.9 2.4 %fusion.55 = f32[2,8,128,128]{2,3,1,0:T(8,128)S(1)} fusion(f32[2,8,128,128]{2,3,1,0:T(8,128)} %get-tuple-element.234, f32[2,8,128,128]{2,3,1,0:T(8,128)S(1)} %copy-done.5, f32[8,128,128]{2,1,0:T(8,128)} %get-tuple-element.233), kind=kOutput, calls=%fused_computation.93 | convolution fusion | flops 402915328 | bytes 3670016 | tf_op jit(solution)/shard_map/hvk,chkl->chvl/dot_general | solution.py:136
  153.4 2.4 %multiply_reduce_fusion = (f32[2,64,8]{1,2,0:T(8,128)S(1)}, f32[2,64,8,128]{3,1,2,0:T(8,128)S(1)}) fusion(f32[2,8,64,128]{3,2,1,0:T(8,128)} %get-tuple-element.228, f32[2,8,64,128]{3,2,1,0:T(8,128)} %get-tuple-element.229, f32[2,8,128,128]{2,3,1,0:T(8,128)S(1)} %fusion.55), kind=kOutput, calls=%fused_computation.109 | convolution fusion | flops 201718784 | bytes 2625536 | tf_op jit(solution)/shard_map/chik,chvk->chiv/dot_general | solution.py:137
  155.8 0.6 copy-done.21
  156.5 1.0 maximum_select_fusion
  157.4 4.5 %collective-permute-start.2 = (bf16[256,256]{1,0:T(8,128)(2,1)S(1)}, bf16[256,256]{1,0:T(8,128)(2,1)S(1)}, u32[]{:S(2)}, u32[]{:S(2)}) collective-permute-start(bf16[256,256]{1,0:T(8,128)(2,1)S(1)} %maximum_select_fusion), channel_id=1, source_target_pairs={{0,8},{4,12},{8,0},{12,4},{1,9},{5,13},{9,1},{13,5},{2,10},{6,14},... | collective-permute-start | bytes 393224 | tf_op jit(solution)/shard_map/ppermute | solution.py:19
  161.9 13.8 %all_gather.3 = bf16[512,256]{1,0:T(8,128)(2,1)S(1)} all-gather(bf16[128,256]{1,0:T(8,128)(2,1)S(1)} %constant_dynamic-slice_fusion.5), channel_id=1, replica_groups=mesh['groups'=2,'seq'=4,'head'=4] {'seq'}, dimensions={0}, use_global_device_ids=true | all-gather | bytes 327680 | tf_op jit(solution)/shard_map/all_gather | solution.py:165
  177.0 0.9 copy-done.23
  177.8 1.2 conditional.1
  178.6 0.5 convolution_add_fusion.1
  179.5 0.7 copy-done.9
  180.3 1.2 multiply_convert_fusion
  (146 shorter events, 8.3 us)
Async XLA Ops:
  0.6 0.9 copy-start
  0.7 6.6 %copy-start.11 = (bf16[128,512]{1,0:T(8,128)(2,1)S(1)}, bf16[128,512]{1,0:T(8,128)(2,1)}, u32[]{:S(2)}) copy-start(bf16[128,512]{1,0:T(8,128)(2,1)} %param.20) | copy-start | bytes 393220
  2.2 154.3 %collective-permute-start.1 = (bf16[128,256]{1,0:T(8,128)(2,1)}, bf16[128,256]{1,0:T(8,128)(2,1)}, u32[]{:S(2)}, u32[]{:S(2)}) collective-permute-start(bf16[128,256]{1,0:T(8,128)(2,1)} %constant_dynamic-slice_fusion.4), channel_id=1, source_target_pairs={{0,4},{4,0},{8,12},{12,8},{1,5},{5,1},{9,13},{13,9},{2,6},{6,2},{1... | collective-permute-start | bytes 196616 | tf_op jit(solution)/shard_map/ppermute | solution.py:19
  5.3 0.7 copy-start.22
  7.8 0.9 copy-start.12
  9.2 1.0 copy-start.8
  10.3 0.7 copy-start.19
  11.0 0.7 copy-start.18
  12.5 0.6 copy-start.24
  12.5 1.8 %copy-start.13 = (f32[2,8,64]{2,0,1:T(2,128)}, f32[2,8,64]{2,0,1:T(2,128)S(1)}, u32[]{:S(2)}) copy-start(f32[2,8,64]{2,0,1:T(2,128)S(1)} %get-tuple-element.591) | copy-start | bytes 12292 | tf_op jit(solution)/shard_map/while
  12.5 44.2 %copy-start.16 = (s32[2,64]{1,0:T(2,128)}, s32[2,64]{1,0:T(2,128)S(1)}, u32[]{:S(2)}) copy-start(s32[2,64]{1,0:T(2,128)S(1)} %get-tuple-element.589) | copy-start | bytes 1540 | tf_op jit(solution)/shard_map/while
  12.5 44.9 %copy-start.1 = (f32[2,8,64,128]{3,1,2,0:T(8,128)}, f32[2,8,64,128]{3,1,2,0:T(8,128)S(1)}, u32[]{:S(2)}) copy-start(f32[2,8,64,128]{3,1,2,0:T(8,128)S(1)} %get-tuple-element.593) | copy-start | bytes 1572868 | tf_op jit(solution)/shard_map/while
  59.8 1.2 copy-start.3
  59.8 1.5 copy-start.6
  61.4 2.1 %copy-start.4 = (f32[2,8,128,128]{2,3,1,0:T(8,128)}, f32[2,8,128,128]{2,3,1,0:T(8,128)S(1)}, u32[]{:S(2)}) copy-start(f32[2,8,128,128]{2,3,1,0:T(8,128)S(1)} %get-tuple-element.586) | copy-start | bytes 3145732 | tf_op jit(solution)/shard_map/while
  61.5 2.1 %copy-start.7 = (f32[2,8,128,128]{2,3,1,0:T(8,128)}, f32[2,8,128,128]{2,3,1,0:T(8,128)S(1)}, u32[]{:S(2)}) copy-start(f32[2,8,128,128]{2,3,1,0:T(8,128)S(1)} %get-tuple-element.587) | copy-start | bytes 3145732 | tf_op jit(solution)/shard_map/while
  65.3 1.1 copy-start.2
  66.4 0.7 copy-start.14
  66.4 0.7 copy-start.17
  66.4 0.7 copy-start.25
  67.1 0.6 copy-start.24
  67.1 1.8 %copy-start.13 = (f32[2,8,64]{2,0,1:T(2,128)}, f32[2,8,64]{2,0,1:T(2,128)S(1)}, u32[]{:S(2)}) copy-start(f32[2,8,64]{2,0,1:T(2,128)S(1)} %get-tuple-element.591) | copy-start | bytes 12292 | tf_op jit(solution)/shard_map/while
  67.1 44.2 %copy-start.16 = (s32[2,64]{1,0:T(2,128)}, s32[2,64]{1,0:T(2,128)S(1)}, u32[]{:S(2)}) copy-start(s32[2,64]{1,0:T(2,128)S(1)} %get-tuple-element.589) | copy-start | bytes 1540 | tf_op jit(solution)/shard_map/while
  67.1 44.9 %copy-start.1 = (f32[2,8,64,128]{3,1,2,0:T(8,128)}, f32[2,8,64,128]{3,1,2,0:T(8,128)S(1)}, u32[]{:S(2)}) copy-start(f32[2,8,64,128]{3,1,2,0:T(8,128)S(1)} %get-tuple-element.593) | copy-start | bytes 1572868 | tf_op jit(solution)/shard_map/while
  114.4 1.2 copy-start.3
  114.4 1.5 copy-start.6
  116.0 2.1 %copy-start.4 = (f32[2,8,128,128]{2,3,1,0:T(8,128)}, f32[2,8,128,128]{2,3,1,0:T(8,128)S(1)}, u32[]{:S(2)}) copy-start(f32[2,8,128,128]{2,3,1,0:T(8,128)S(1)} %get-tuple-element.586) | copy-start | bytes 3145732 | tf_op jit(solution)/shard_map/while
  116.0 2.1 %copy-start.7 = (f32[2,8,128,128]{2,3,1,0:T(8,128)}, f32[2,8,128,128]{2,3,1,0:T(8,128)S(1)}, u32[]{:S(2)}) copy-start(f32[2,8,128,128]{2,3,1,0:T(8,128)S(1)} %get-tuple-element.587) | copy-start | bytes 3145732 | tf_op jit(solution)/shard_map/while
  119.8 1.1 copy-start.2
  120.9 0.7 copy-start.14
  120.9 0.7 copy-start.17
  120.9 0.7 copy-start.25
  122.1 28.8 %copy-start.5 = (f32[2,8,128,128]{2,3,1,0:T(8,128)S(1)}, f32[2,8,128,128]{2,3,1,0:T(8,128)}, u32[]{:S(2)}) copy-start(f32[2,8,128,128]{2,3,1,0:T(8,128)} %get-tuple-element.230) | copy-start | bytes 3145732
  122.1 7.6 %collective-permute-start = (bf16[8,128,128]{2,1,0:T(8,128)(2,1)S(1)}, bf16[8,128,128]{2,1,0:T(8,128)(2,1)S(1)}, u32[]{:S(2)}, u32[]{:S(2)}) collective-permute-start(bf16[8,128,128]{2,1,0:T(8,128)(2,1)S(1)} %get-tuple-element.606), channel_id=1, source_target_pairs={{0,4},{4,8},{8,12},{1,5},{5,9},{9,13},{2,6},{6,10},{10,14},{3,7},{... | collective-permute-start | bytes 786440 | tf_op jit(solution)/shard_map/while/body/eval_jaxpr/ppermute | solution.py:30
  130.9 9.2 %collective-permute-start = (bf16[8,128,128]{2,1,0:T(8,128)(2,1)S(1)}, bf16[8,128,128]{2,1,0:T(8,128)(2,1)S(1)}, u32[]{:S(2)}, u32[]{:S(2)}) collective-permute-start(bf16[8,128,128]{2,1,0:T(8,128)(2,1)S(1)} %get-tuple-element.606), channel_id=1, source_target_pairs={{0,4},{4,8},{8,12},{1,5},{5,9},{9,13},{2,6},{6,10},{10,14},{3,7},{... | collective-permute-start | bytes 786440 | tf_op jit(solution)/shard_map/while/body/eval_jaxpr/ppermute | solution.py:30
  141.4 8.3 %collective-permute-start = (bf16[8,128,128]{2,1,0:T(8,128)(2,1)S(1)}, bf16[8,128,128]{2,1,0:T(8,128)(2,1)S(1)}, u32[]{:S(2)}, u32[]{:S(2)}) collective-permute-start(bf16[8,128,128]{2,1,0:T(8,128)(2,1)S(1)} %get-tuple-element.606), channel_id=1, source_target_pairs={{0,4},{4,8},{8,12},{1,5},{5,9},{9,13},{2,6},{6,10},{10,14},{3,7},{... | collective-permute-start | bytes 786440 | tf_op jit(solution)/shard_map/while/body/eval_jaxpr/ppermute | solution.py:30
  153.4 3.1 %copy-start.15 = (bf16[128,512]{1,0:T(8,128)(2,1)S(1)}, bf16[128,512]{1,0:T(8,128)(2,1)}, u32[]{:S(2)}) copy-start(bf16[128,512]{1,0:T(8,128)(2,1)} %param.27) | copy-start | bytes 393220
  155.8 0.7 copy-start.21
  157.4 19.5 %collective-permute-start.2 = (bf16[256,256]{1,0:T(8,128)(2,1)S(1)}, bf16[256,256]{1,0:T(8,128)(2,1)S(1)}, u32[]{:S(2)}, u32[]{:S(2)}) collective-permute-start(bf16[256,256]{1,0:T(8,128)(2,1)S(1)} %maximum_select_fusion), channel_id=1, source_target_pairs={{0,8},{4,12},{8,0},{12,4},{1,9},{5,13},{9,1},{13,5},{2,10},{6,14},... | collective-permute-start | bytes 393224 | tf_op jit(solution)/shard_map/ppermute | solution.py:19
  176.9 1.0 copy-start.23
  176.9 0.9 copy-start.20
  179.3 1.0 copy-start.9
  179.3 1.0 copy-start.10
